TPU v7x, 512 devices: a whole 4x8x8 slice. The times are simulated.
512 devices in a mesh: seq: 64 (over z, x, core), head: 8 (over y).
Axes of the slice: x: 4, y: 8, z: 8, core: 2. Of those that a mesh axis runs over, the one named last changes fastest.
Arguments:
- xbc: bfloat16 [24576, 10240], P('seq', 'head'), may hold values from -6 to 6
- gate_z: bfloat16 [24576, 8192], P('seq', 'head'), may hold values from -6 to 6
- dt_raw: bfloat16 [128, 24576], P('head', 'seq'), may hold values from -3 to 3
- dt_bias: float32 [128], P('head'), may hold values from -1 to 0.5
- a_log: float32 [128], P('head'), may hold values from -11.5 to -6.6
- skip_d: float32 [128], P('head'), may hold values from 0.5 to 1.5
- conv_weight: float32 [4, 10240], P(None, 'head'), may hold values from -3 to 3
- conv_bias: float32 [10240], P('head'), may hold values from -3 to 3
- norm_gain: float32 [8192], P('head'), may hold values from 0.1 to 1.9
- out_weight: bfloat16 [8192, 4096], P('head', 'seq'), may hold values from -0.1875 to 0.1875
- starts: int32 [24576], P('seq'), may hold values from 0 to 1, as said below
Outputs:
- mixed: bfloat16 [24576, 4096], P('seq', 'head')
Inputs may be any that keep to these rules, and one draw needn't show every extreme that they name: `starts`: a 0 or 1 flag for every token; every 1 lies among the first 6144 tokens, and there is at least one.
All inputs are finite; a program needn't handle non-finite values.
Results may differ from a plain program's by a relative error of at most 0.013.
Values may be sent and summed in bfloat16 or wider, within the bound.
A program may use at most 128 MiB of HBM per device.

v0:
```python
import jax
import jax.numpy as jnp
from jax import lax
from jax.sharding import PartitionSpec as P

P_SIZE = 64
N = 128
DI = 8192
HG = 16
GW = 1280


def carried_in(part, axis, combine, identity):
    place = lax.axis_index(axis)
    gathered = jax.tree.map(lambda a: lax.all_gather(a, axis), part)
    state = jax.tree.map(lambda a, e: jnp.zeros_like(a) + jnp.asarray(e, a.dtype), part, identity)

    def one(hop, state):
        return combine(
            state, jax.tree.map(lambda a: lax.dynamic_index_in_dim(a, hop, 0, False), gathered)
        )

    return lax.fori_loop(0, place, one, state)


def passed_along(block, axis, distance):
    devices = range(lax.axis_size(axis))
    route = [(i - distance, i) for i in devices if i - distance in devices]
    return lax.ppermute(block, axis, route)


def combine(earlier, later):
    return (earlier[0] * later[0], later[0][:, None, None] * earlier[1] + later[1])


def chain_states(decays, states):
    identity = (jnp.ones_like(decays), jnp.zeros_like(states))
    result = carried_in((decays, states), "seq", combine, identity)
    return result[1]


def block_local(item):
    xc, bc, cc, dtc, lc, sc = item
    cumul = jnp.cumsum(lc, axis=1)
    runs = jnp.cumsum(sc)
    tail = (
        jnp.where(
            (runs == runs[-1])[None, :], jnp.exp(jnp.minimum(cumul[:, -1:] - cumul, 0.0)), 0.0
        )
        * dtc
    )
    b_heads = jnp.repeat(bc, HG, axis=1)
    scaled = (tail[:, :, None] * jnp.swapaxes(b_heads, 0, 1).astype(jnp.float32)).astype(
        jnp.bfloat16
    )
    local = jnp.einsum("shp,hsn->hpn", xc, scaled, preferred_element_type=jnp.float32)
    total = jnp.exp(cumul[:, -1]) * (runs[-1] == 0).astype(jnp.float32)
    enter = jnp.exp(cumul) * (runs == 0).astype(jnp.float32)[None, :]
    return (local, total, enter)


def block_inner(item):
    xc, bc, cc, dtc, lc, sc = item
    length = xc.shape[0]
    cumul = jnp.cumsum(lc, axis=1)
    runs = jnp.cumsum(sc)
    lower = jnp.arange(length)[:, None] >= jnp.arange(length)[None, :]
    same = lower & (runs[:, None] == runs[None, :])
    diff = cumul[:, :, None] - cumul[:, None, :]
    wdec = jnp.where(same[None], jnp.exp(jnp.minimum(diff, 0.0)), 0.0)
    scores = jnp.einsum("tgn,sgn->gts", cc, bc, preferred_element_type=jnp.float32)
    scores_h = jnp.repeat(scores, HG, axis=0)
    weights = (scores_h * wdec * dtc[:, None, :]).astype(jnp.bfloat16)
    return jnp.einsum("hts,shp->thp", weights, xc, preferred_element_type=jnp.float32)


def body(
    xbc,
    gate_z,
    dt_raw,
    dt_bias,
    a_log,
    skip_d,
    conv_weight,
    conv_bias,
    norm_gain,
    out_weight,
    starts,
):
    tok = xbc.shape[0]
    width = conv_weight.shape[0]
    chans = xbc.shape[1]
    groups = chans // GW
    heads = dt_raw.shape[0]
    rim, rim_flags = passed_along(
        (xbc[tok - (width - 1) :], starts[tok - (width - 1) :].astype(jnp.bfloat16)), "seq", 1
    )
    flags_int = rim_flags.astype(jnp.int32)
    after_rim = jnp.sum(flags_int) - jnp.cumsum(flags_int)
    counts = jnp.cumsum(starts)
    padded = jnp.concatenate([rim, xbc], axis=0).astype(jnp.float32)
    count_ext = jnp.concatenate([-after_rim, counts])
    acc = conv_bias[None, :] + conv_weight[width - 1][None, :] * xbc.astype(jnp.float32)
    for lag in range(1, width):
        shifted = padded[width - 1 - lag : width - 1 - lag + tok]
        keep = (count_ext[width - 1 - lag : width - 1 - lag + tok] == counts).astype(jnp.float32)
        acc = acc + conv_weight[width - 1 - lag][None, :] * shifted * keep[:, None]
    unit = jax.nn.silu(acc).astype(jnp.bfloat16)
    grid = unit.reshape(tok, groups, GW)
    xs = grid[:, :, : HG * P_SIZE].reshape(tok, heads, P_SIZE)
    bmat = grid[:, :, HG * P_SIZE : HG * P_SIZE + N]
    cmat = grid[:, :, HG * P_SIZE + N :]
    steps_dt = jax.nn.softplus(dt_raw.astype(jnp.float32) + dt_bias[:, None])
    logs = -jnp.exp(a_log)[:, None] * steps_dt
    length = min(128, tok)
    nblocks = tok // length
    x_blocks = xs.reshape(nblocks, length, heads, P_SIZE)
    b_blocks = bmat.reshape(nblocks, length, groups, N)
    c_blocks = cmat.reshape(nblocks, length, groups, N)
    dt_blocks = steps_dt.reshape(heads, nblocks, length).transpose(1, 0, 2)
    log_blocks = logs.reshape(heads, nblocks, length).transpose(1, 0, 2)
    start_blocks = starts.reshape(nblocks, length)
    items = (x_blocks, b_blocks, c_blocks, dt_blocks, log_blocks, start_blocks)

    def fold(carry, item):
        local, total = item
        return ((carry[0] * total, carry[1] * total[:, None, None] + local), None)

    y_diag, (locals_all, totals, enters) = lax.map(
        lambda item: (block_inner(item), block_local(item)), items
    )
    init = (jnp.ones((heads,), jnp.float32), jnp.zeros((heads, P_SIZE, N), jnp.float32))
    result, unused = lax.scan(fold, init, (locals_all, totals))
    entering = chain_states(result[0], result[1])

    def apply(state, item):
        cc, enter, local, total = item
        c_heads = jnp.repeat(cc, HG, axis=1)
        y_off = (
            jnp.einsum(
                "thn,hpn->thp",
                c_heads,
                state.astype(jnp.bfloat16),
                preferred_element_type=jnp.float32,
            )
            * enter.T[:, :, None]
        )
        return (state * total[:, None, None] + local, y_off)

    unused_state, y_offs = lax.scan(apply, entering, (c_blocks, enters, locals_all, totals))
    y_all = (y_diag + y_offs).reshape(tok, heads, P_SIZE) + skip_d[None, :, None] * xs.astype(
        jnp.float32
    )
    gated = y_all.reshape(tok, heads * P_SIZE) * jax.nn.silu(gate_z.astype(jnp.float32))
    total_sq = lax.psum(jnp.sum(gated * gated, axis=1), "head")
    normed = (gated * lax.rsqrt(total_sq / DI + 1e-05)[:, None] * norm_gain[None, :]).astype(
        jnp.bfloat16
    )
    terms = jnp.dot(
        normed,
        lax.all_gather(out_weight, "seq", axis=1, tiled=True),
        preferred_element_type=jnp.float32,
    )
    return lax.psum_scatter(terms.astype(jnp.bfloat16), "head", scatter_dimension=1, tiled=True)


def solution(mesh):
    placed = (
        P("seq", "head"),
        P("seq", "head"),
        P("head", "seq"),
        P("head"),
        P("head"),
        P("head"),
        P(None, "head"),
        P("head"),
        P("head"),
        P("head", "seq"),
        P("seq"),
    )
    return jax.shard_map(
        body, mesh=mesh, in_specs=placed, out_specs=P("seq", "head"), check_vma=False
    )
```

profile of v0, /device:TPU:2, one launch (start us, length us, event | category | flops | bytes accessed | tf_op | source)
XLA Modules:
  0.0 368.8 jit_solution(15041050396364430548)
XLA Ops:
  7.3 1.9 collective-permute-start.1
  10.0 3.5 collective-permute-start
  19.0 1.4 maximum_convert_fusion
  20.5 1.9 fusion.44
  23.3 1.9 reshape.277
  25.2 2.0 copy.38
  27.2 1.3 broadcast.139.clone
  28.5 17.6 %while.53 = (s32[]{:T(128)}, f32[3,128,16,64]{1,3,2,0:T(8,128)}, f32[3,16,64,128]{3,2,1,0:T(8,128)S(1)}, f32[3,16]{1,0:T(4,128)S(1)}, f32[3,16,128]{2,1,0:T(8,12...) while((s32[]{:T(128)}, f32[3,128,16,64]{1,3,2,0:T(8,128)}, ...), condition=%wide.region_7.8_spmd, body=%wide.region_4.7_spmd.sunk | while | flops 73752848 | bytes 2099011 | solution.py:129
  33.0 1.4 fusion.75
  38.9 1.4 fusion.75
  44.7 1.4 fusion.75
  50.7 130.2 %all-reduce = f32[1024]{0:T(1024)S(1)} all-reduce(f32[1024]{0:T(1024)S(1)} %dynamic-update-slice), channel_id=2, replica_groups=mesh['seq'=64,'head'=8] {'seq'}, use_global_device_ids=true, to_apply=%add | all-reduce | flops 1024 | bytes 8192
  181.0 18.2 %all-gather.7.cloned.1.call-done = f32[1024,64,128]{2,1,0:T(8,128)} async-done(((f32[16,64,128]{2,1,0:T(8,128)}), f32[1024,64,128]{2,1,0:T(8,128)}) %all-gather.7.cloned.1.call-update) | async-done | bytes 33554448 | tf_op jit(solution)/shard_map/all_gather | solution.py:15
  199.3 2.5 while.54
  201.7 1.3 broadcast.139
  203.1 4.4 %while.55 = (s32[]{:T(128)}, f32[16,64,128]{2,1,0:T(8,128)S(1)}, f32[3,128,16,64]{1,3,2,0:T(8,128)}, f32[3,16]{1,0:T(4,128)S(1)}, f32[3,16,64,128]{3,2,1,0:T(8,1...) while((s32[]{:T(128)}, f32[16,64,128]{2,1,0:T(8,128)S(1)}, ...), condition=%wide.region_13.14_spmd, body=%wide.region_12.13_spmd.sunk | while | flops 34078720 | bytes 2745125 | solution.py:150
  207.5 3.4 add.93
  210.9 2.3 copy.48
  213.2 1.8 reshape.278
  215.0 2.6 multiply_reduce_fusion.1
  217.6 17.0 %psum.7 = f32[384]{0:T(512)S(1)} all-reduce(f32[384]{0:T(512)S(1)} %get-tuple-element.329), channel_id=1, replica_groups=mesh['seq'=64,'head'=8] {'head'}, use_global_device_ids=true, to_apply=%region_15.16 | all-reduce | flops 384 | bytes 3072 | tf_op jit(solution)/shard_map/psum | solution.py:155
  234.6 53.6 %all-gather.5.cloned.1.call-done = bf16[1024,4096]{0,1:T(8,128)(2,1)} async-done(((bf16[1024,64]{0,1:T(8,128)(2,1)}), bf16[1024,4096]{0,1:T(8,128)(2,1)}) %all-gather.5.cloned.1.call-update) | async-done | bytes 8388624 | tf_op jit(solution)/shard_map/all_gather | solution.py:161
  288.3 10.2 %convolution_convert_fusion = bf16[384,4096]{1,0:T(8,128)(2,1)} fusion(bf16[1024,4096]{0,1:T(8,128)(2,1)} %all-gather.5.cloned.1.call-done, f32[384,1024]{1,0:T(8,128)S(1)} %get-tuple-element.330, f32[1024]{0:T(1024)S(1)} %copy-done.5, f32[384]{0:T(512)S(1)} %add_rsqrt_fusion), kind=kOutput, calls=%fused_computation.59 | convolution fusion | flops 3223977984 | bytes 13112832 | tf_op jit(solution)/shard_map/dot_general | solution.py:159
  298.5 63.8 %reduce-scatter.2.cloned.1.call-done = bf16[384,512]{1,0:T(8,128)(2,1)} async-done(((bf16[384,4096]{1,0:T(8,128)(2,1)}), bf16[384,512]{1,0:T(8,128)(2,1)}) %reduce-scatter.2.cloned.1.call-update) | async-done | bytes 393232 | tf_op jit(solution)/shard_map/reduce_scatter | solution.py:164
  (128 shorter events, 30.2 us)
Async XLA Ops:
  6.5 192.7 %all-gather.7.cloned.1.call-start = ((), (), s32[]{:S(2)}) async-start(), calls=%async_computation.3 | async-start | bytes 34078720 | tf_op jit(solution)/shard_map/all_gather | solution.py:15
  7.3 10.0 %collective-permute-start.1 = (bf16[3]{0:T(256)(128)(2,1)S(1)}, bf16[3]{0:T(256)(128)(2,1)S(1)}, u32[]{:S(2)}, u32[]{:S(2)}) collective-permute-start(bf16[3]{0:T(256)(128)(2,1)S(1)} %slice.68), channel_id=1, source_target_pairs={{0,8},{8,16},{16,24},{24,32},{32,40},{40,48},{48,56},{56,64},{64,7... | collective-permute-start | bytes 26 | tf_op jit(solution)/shard_map/ppermute | solution.py:29
  10.0 9.1 %collective-permute-start = (bf16[3,1280]{1,0:T(4,128)(2,1)S(1)}, bf16[3,1280]{1,0:T(4,128)(2,1)S(1)}, u32[]{:S(2)}, u32[]{:S(2)}) collective-permute-start(bf16[3,1280]{1,0:T(4,128)(2,1)S(1)} %slice.66), channel_id=1, source_target_pairs={{0,8},{8,16},{16,24},{24,32},{32,40},{40,48},{48,56},{56,64},{64,7... | collective-permute-start | bytes 23048 | tf_op jit(solution)/shard_map/ppermute | solution.py:29
  17.2 3.2 copy-start.2
  17.2 3.2 copy-start.3
  22.3 1.0 copy-start.1
  46.1 2.1 copy-start.4
  46.6 0.8 copy-start
  47.5 240.8 %all-gather.5.cloned.1.call-start = ((), (), s32[]{:S(2)}) async-start(), calls=%async_computation.1 | async-start | bytes 8519680 | tf_op jit(solution)/shard_map/all_gather | solution.py:161
  48.2 314.0 %reduce-scatter.2.cloned.1.call-start = ((), (), s32[]{:S(2)}) async-start(), calls=%async_computation.2 | async-start | bytes 3538944 | tf_op jit(solution)/shard_map/reduce_scatter | solution.py:164
  215.0 73.2 %copy-start.5 = (f32[1024]{0:T(1024)S(1)}, f32[1024]{0:T(1024)}, u32[]{:S(2)}) copy-start(f32[1024]{0:T(1024)} %param.27) | copy-start | bytes 12292
Sparse Core Ops, SparseCore 0:
  47.6 151.5 all-gather.6
  202.6 85.6 all-gather.4
  298.6 63.6 reduce-scatter.1
where the time goes:
time: 372 us; the launch traced here: 369 us
  blocking collectives  147 us (40%)
  waiting for transfers between devices  136 us (37%)
  other arithmetic  22.4 us (6%)
  local copies, waits for them, and re-layouts  20.7 us (6%)
  matrix products  20.1 us (5%)
  between operations  14 us (4%)
  starting transfers between devices  5.48 us (1%)
    unnamed x1, blocking collectives  130 us
    reduce_scatter x1, waiting for transfers between devices, body(): lax.psum_scatter(terms.astype(jnp.bfloat16), 'head', scatter_dimension=1,...  63.8 us
    all_gather x1, waiting for transfers between devices, body(): lax.all_gather(out_weight, 'seq', axis=1, tiled=True)  53.6 us
    all_gather x1, waiting for transfers between devices, carried_in(): gathered = jax.tree.map(lambda a: lax.all_gather(a, axis), part)  18.2 us
    psum x1, blocking collectives, body(): total_sq = lax.psum(jnp.sum(gated * gated, axis=1), 'head')  17 us
    dot_general x1, matrix products, body(): jnp.dot(normed, lax.all_gather(out_weight, 'seq', axis=1, tiled=True), pr...  10.2 us
  transfers between devices with their start and end apart: 5, of which 3 were waited for; matrix products, arithmetic and copies ran while one was open for 7% of the time, Pallas kernels for 0%

commit v1 on v0

--- a/solution.py
+++ b/solution.py
@@ -152,7 +152,9 @@
         jnp.float32
     )
     gated = y_all.reshape(tok, heads * P_SIZE) * jax.nn.silu(gate_z.astype(jnp.float32))
-    total_sq = lax.psum(jnp.sum(gated * gated, axis=1), "head")
+    block_2 = jnp.sum(gated * gated, axis=1)
+    pieces = lax.all_gather(block_2, "head", axis=0, tiled=False)
+    total_sq = pieces.sum(axis=0)
     normed = (gated * lax.rsqrt(total_sq / DI + 1e-05)[:, None] * norm_gain[None, :]).astype(
         jnp.bfloat16
     )

time: 372 us -> 379 us (1.019)
  the two profiles are of different devices: /device:TPU:2 before, /device:TPU:6 now
where the time goes in v1:
time: 379 us; the launch traced here: 375 us
  blocking collectives  143 us (38%)
  waiting for transfers between devices  141 us (37%)
  other arithmetic  27.1 us (7%)
  local copies, waits for them, and re-layouts  20.7 us (5%)
  matrix products  20.1 us (5%)
  between operations  14.1 us (4%)
  starting transfers between devices  6.28 us (2%)
    unnamed x1, blocking collectives  119 us
    reduce_scatter x1, waiting for transfers between devices, body(): lax.psum_scatter(terms.astype(jnp.bfloat16), 'head', scatter_dimension=1,...  70.7 us
    all_gather x1, waiting for transfers between devices, body(): lax.all_gather(out_weight, 'seq', axis=1, tiled=True)  41.7 us
    all_gather x1, waiting for transfers between devices, carried_in(): gathered = jax.tree.map(lambda a: lax.all_gather(a, axis), part)  27.7 us
    all_gather x1, blocking collectives, body(): pieces = lax.all_gather(block_2, 'head', axis=0, tiled=False)  23.8 us
    dot_general x1, matrix products, body(): jnp.dot(normed, lax.all_gather(out_weight, 'seq', axis=1, tiled=True), pr...  10.2 us
  transfers between devices with their start and end apart: 5, of which 3 were waited for; matrix products, arithmetic and copies ran while one was open for 8% of the time, Pallas kernels for 0%

profile of v1, /device:TPU:6, one launch (start us, length us, event | category | flops | bytes accessed | tf_op | source)
XLA Modules:
  0.0 375.0 jit_solution(14710446757673591819)
XLA Ops:
  7.3 1.9 collective-permute-start.1
  10.0 4.3 %collective-permute-start = (bf16[3,1280]{1,0:T(4,128)(2,1)S(1)}, bf16[3,1280]{1,0:T(4,128)(2,1)S(1)}, u32[]{:S(2)}, u32[]{:S(2)}) collective-permute-start(bf16[3,1280]{1,0:T(4,128)(2,1)S(1)} %slice.66), channel_id=1, source_target_pairs={{0,8},{8,16},{16,24},{24,32},{32,40},{40,48},{48,56},{56,64},{64,7... | collective-permute-start | bytes 23048 | tf_op jit(solution)/shard_map/ppermute | solution.py:29
  19.8 1.4 maximum_convert_fusion
  21.3 1.9 fusion.44
  24.1 1.9 reshape.285
  26.0 2.0 copy.38
  28.0 1.3 broadcast.146.clone
  29.3 17.6 %while.53 = (s32[]{:T(128)}, f32[3,128,16,64]{1,3,2,0:T(8,128)}, f32[3,16,64,128]{3,2,1,0:T(8,128)S(1)}, f32[3,16]{1,0:T(4,128)S(1)}, f32[3,16,128]{2,1,0:T(8,12...) while((s32[]{:T(128)}, f32[3,128,16,64]{1,3,2,0:T(8,128)}, ...), condition=%wide.region_7.8_spmd, body=%wide.region_4.7_spmd.sunk | while | flops 73752848 | bytes 2099011 | solution.py:129
  33.8 1.4 fusion.75
  39.7 1.4 fusion.75
  45.5 1.4 fusion.75
  51.5 119.4 %all-reduce = f32[1024]{0:T(1024)S(1)} all-reduce(f32[1024]{0:T(1024)S(1)} %dynamic-update-slice), channel_id=2, replica_groups=mesh['seq'=64,'head'=8] {'seq'}, use_global_device_ids=true, to_apply=%add | all-reduce | flops 1024 | bytes 8192
  171.0 27.7 %all-gather.9.cloned.1.call-done = f32[1024,64,128]{2,1,0:T(8,128)} async-done(((f32[16,64,128]{2,1,0:T(8,128)}), f32[1024,64,128]{2,1,0:T(8,128)}) %all-gather.9.cloned.1.call-update) | async-done | bytes 33554448 | tf_op jit(solution)/shard_map/all_gather | solution.py:15
  198.7 7.4 %while.54 = (s32[]{:T(128)}, f32[16,64,128]{2,1,0:T(8,128)S(1)}, s32[]{:T(128)}, f32[64,16]{1,0:T(8,128)S(1)}, f32[64,16,64,128]{3,2,1,0:T(8,128)}, /*index=5*/s32[]{:T(128)}, s32[]{:T(128)}, s32[]{:T(128)}) while((s32[]{:T(128)}, f32[16,64,128]{2,1,0:T(8,128)S(1)}, s32[]{:T(128)}, f32[64,16]{1,0:T(8,128)S(1)}, ...), condition=%wide.region_11.12_spmd, body=%wide.region_10.11_spmd.sunk | while | flops 262149 | bytes 1573183 | solution.py:23
  206.1 1.3 broadcast.146
  207.5 4.4 %while.55 = (s32[]{:T(128)}, f32[16,64,128]{2,1,0:T(8,128)S(1)}, f32[3,128,16,64]{1,3,2,0:T(8,128)}, f32[3,16]{1,0:T(4,128)S(1)}, f32[3,16,64,128]{3,2,1,0:T(8,1...) while((s32[]{:T(128)}, f32[16,64,128]{2,1,0:T(8,128)S(1)}, ...), condition=%wide.region_13.14_spmd, body=%wide.region_12.13_spmd.sunk | while | flops 34078720 | bytes 2745125 | solution.py:150
  211.9 3.4 add.95
  215.3 2.3 copy.48
  217.6 1.8 reshape.286
  219.4 2.5 multiply_reduce_fusion.1
  222.0 23.8 %all-gather.3 = f32[8,1,384]{2,1,0:T(1,128)S(1)} all-gather(f32[1,1,384]{2,1,0:T(1,128)S(1)} %reshape.280), channel_id=4, replica_groups=mesh['seq'=64,'head'=8] {'head'}, dimensions={0}, use_global_device_ids=true | all-gather | bytes 13824 | tf_op jit(solution)/shard_map/all_gather | solution.py:156
  245.9 41.7 %all-gather.7.cloned.1.call-done = bf16[1024,4096]{0,1:T(8,128)(2,1)} async-done(((bf16[1024,64]{0,1:T(8,128)(2,1)}), bf16[1024,4096]{0,1:T(8,128)(2,1)}) %all-gather.7.cloned.1.call-update) | async-done | bytes 8388624 | tf_op jit(solution)/shard_map/all_gather | solution.py:163
  287.6 10.2 %convolution_convert_fusion = bf16[384,4096]{1,0:T(8,128)(2,1)} fusion(bf16[1024,4096]{0,1:T(8,128)(2,1)} %all-gather.7.cloned.1.call-done, f32[384,1024]{1,0:T(8,128)S(1)} %get-tuple-element.330, f32[1024]{0:T(1024)S(1)} %copy-done.5, f32[384]{0:T(512)S(1)} %add_rsqrt_fusion), kind=kOutput, calls=%fused_computation.59 | convolution fusion | flops 3223977984 | bytes 13112832 | tf_op jit(solution)/shard_map/dot_general | solution.py:161
  297.8 70.7 %reduce-scatter.2.cloned.1.call-done = bf16[384,512]{1,0:T(8,128)(2,1)} async-done(((bf16[384,4096]{1,0:T(8,128)(2,1)}), bf16[384,512]{1,0:T(8,128)(2,1)}) %reduce-scatter.2.cloned.1.call-update) | async-done | bytes 393232 | tf_op jit(solution)/shard_map/reduce_scatter | solution.py:166
  (138 shorter events, 35.1 us)
Async XLA Ops:
  6.5 192.1 %all-gather.9.cloned.1.call-start = ((), (), s32[]{:S(2)}) async-start(), calls=%async_computation.3 | async-start | bytes 34078720 | tf_op jit(solution)/shard_map/all_gather | solution.py:15
  7.3 10.8 %collective-permute-start.1 = (bf16[3]{0:T(256)(128)(2,1)S(1)}, bf16[3]{0:T(256)(128)(2,1)S(1)}, u32[]{:S(2)}, u32[]{:S(2)}) collective-permute-start(bf16[3]{0:T(256)(128)(2,1)S(1)} %slice.68), channel_id=1, source_target_pairs={{0,8},{8,16},{16,24},{24,32},{32,40},{40,48},{48,56},{56,64},{64,7... | collective-permute-start | bytes 26 | tf_op jit(solution)/shard_map/ppermute | solution.py:29
  10.0 9.9 %collective-permute-start = (bf16[3,1280]{1,0:T(4,128)(2,1)S(1)}, bf16[3,1280]{1,0:T(4,128)(2,1)S(1)}, u32[]{:S(2)}, u32[]{:S(2)}) collective-permute-start(bf16[3,1280]{1,0:T(4,128)(2,1)S(1)} %slice.66), channel_id=1, source_target_pairs={{0,8},{8,16},{16,24},{24,32},{32,40},{40,48},{48,56},{56,64},{64,7... | collective-permute-start | bytes 23048 | tf_op jit(solution)/shard_map/ppermute | solution.py:29
  18.0 3.2 copy-start.2
  18.0 3.2 copy-start.3
  23.1 1.0 copy-start.1
  46.9 2.1 copy-start.4
  47.4 0.8 copy-start
  48.3 239.3 %all-gather.7.cloned.1.call-start = ((), (), s32[]{:S(2)}) async-start(), calls=%async_computation.1 | async-start | bytes 8519680 | tf_op jit(solution)/shard_map/all_gather | solution.py:163
  49.0 319.5 %reduce-scatter.2.cloned.1.call-start = ((), (), s32[]{:S(2)}) async-start(), calls=%async_computation.2 | async-start | bytes 3538944 | tf_op jit(solution)/shard_map/reduce_scatter | solution.py:166
  219.4 68.2 %copy-start.5 = (f32[1024]{0:T(1024)S(1)}, f32[1024]{0:T(1024)}, u32[]{:S(2)}) copy-start(f32[1024]{0:T(1024)} %param.27) | copy-start | bytes 12292
Sparse Core Ops, SparseCore 0:
  48.4 150.2 all-gather.8
  202.0 85.5 all-gather.6
  297.9 70.5 reduce-scatter.1
